TPU v7x, 32 devices: a whole 2x2x4 slice. The times are simulated.
32 devices in a mesh: band: 4 (over y, x), query: 8 (over z, core).
Axes of the slice: x: 2, y: 2, z: 4, core: 2. Of those that a mesh axis runs over, the one named last changes fastest.
Arguments:
- spectra: bfloat16 [192, 20480], P('band'), may hold values from 0 to 3
- theo: bfloat16 [8, 8, 20480], P('query', 'band'), may hold values from -0.0390625 to 0.0390625
- offsets: int32 [16], replicated, may hold values from -128 to 128
- win_lo: int32 [192], P('band'), may hold values from 0 to 32
- win_len: int32 [192], P('band'), may hold values from 1 to 32
Outputs:
- best: float32 [192, 16], P(('band', 'query'))
- average: float32 [192, 16], P(('band', 'query'))
Inputs may be any that keep to these rules, and one draw needn't show every extreme that they name: win_lo + win_len never exceeds 64.
All inputs are finite; a program needn't handle non-finite values.
Results may differ from a plain program's by a relative error of at most 0.003.
Values may be sent and summed in bfloat16 or wider, within the bound.
A program may use at most 128 MiB of HBM per device.

v0:
```python
import jax
import jax.numpy as jnp
from jax import lax
from jax.sharding import PartitionSpec as P

BG_HALF = 75
SHIFT_MAX = 128


def box_table():
    source = lax.broadcasted_iota(jnp.int32, (384, 128), 0)
    target = lax.broadcasted_iota(jnp.int32, (384, 128), 1)
    offset_gap = source - 128 - target
    inside = (jnp.abs(offset_gap) <= BG_HALF) & (offset_gap != 0)
    return inside.astype(jnp.bfloat16)


def correct(intensity):
    row_count, bin_count = intensity.shape
    block_count = bin_count // 128
    blocks = intensity.reshape(row_count, block_count, 128)
    zero_block = jnp.zeros((row_count, 1, 128), intensity.dtype)
    previous = jnp.concatenate([zero_block, blocks[:, :-1]], axis=1)
    following = jnp.concatenate([blocks[:, 1:], zero_block], axis=1)
    stacked = jnp.concatenate([previous, blocks, following], axis=2)
    window_sum = jnp.einsum("rbj,ji->rbi", stacked, box_table(), preferred_element_type=jnp.float32)
    result = blocks.astype(jnp.float32) - window_sum / (2.0 * BG_HALF)
    return result.astype(jnp.bfloat16).reshape(row_count, bin_count)


def shifted_copies(peptides, offsets):
    bin_count = peptides.shape[1]
    padded = jnp.pad(peptides, ((0, 0), (SHIFT_MAX, SHIFT_MAX)))

    def take_shift(offset):
        return lax.dynamic_slice_in_dim(padded, SHIFT_MAX - offset, bin_count, 1)

    copies = jax.vmap(take_shift, out_axes=1)(offsets)
    return copies.reshape(-1, bin_count)


def local(spectra, theo, offsets, win_lo, win_len):
    query_count = lax.axis_size("query")
    spectra_rows = spectra.shape[0]
    own_rows = spectra_rows // query_count
    own_start = lax.axis_index("query") * own_rows
    corrected = correct(spectra)
    shift_count = offsets.shape[0]
    group_size = theo.shape[1] * lax.axis_size("band")
    piece = lax.all_gather(theo, "band", axis=1, tiled=True)
    piece_rows = piece.shape[1]
    copies = shifted_copies(piece[0], offsets)
    partial_scores = jnp.einsum("mb,sb->ms", copies, corrected, preferred_element_type=jnp.float32)
    scores = partial_scores.reshape(1, piece_rows, shift_count * spectra_rows)
    score_table = scores.reshape(group_size, shift_count, query_count, own_rows)
    low_own = lax.dynamic_slice_in_dim(win_lo, own_start, own_rows, 0)
    length_own = lax.dynamic_slice_in_dim(win_len, own_start, own_rows, 0)
    gathered = lax.all_to_all(score_table, "query", split_axis=2, concat_axis=0, tiled=True)
    total_peptides = gathered.shape[0]
    owned_scores = gathered.reshape(total_peptides, shift_count, own_rows)
    peptide_index = lax.broadcasted_iota(jnp.int32, (total_peptides, own_rows), 0)
    inside = (peptide_index >= low_own[None, :]) & (peptide_index < (low_own + length_own)[None, :])
    best_score = jnp.max(jnp.where(inside[:, None, :], owned_scores, -jnp.inf), axis=0).T
    totals = jnp.sum(jnp.where(inside[:, None, :], owned_scores, 0.0), axis=0).T
    average = totals / length_own[:, None].astype(jnp.float32)
    return (best_score, average)


def solution(mesh):
    placed = (P("band", None), P("query", "band", None), P(), P("band"), P("band"))
    return jax.shard_map(
        local,
        mesh=mesh,
        in_specs=placed,
        out_specs=(P(("band", "query"), None), P(("band", "query"), None)),
        check_vma=False,
    )
```

profile of v0, /device:TPU:0, one launch (start us, length us, event | category | flops | bytes accessed | tf_op | source)
XLA Modules:
  0.0 84.9 jit_solution(6701654885838280901)
XLA Ops:
  0.7 1.2 %copy.17 = bf16[1,2,20480]{2,0,1:T(2,128)(2,1)S(1)} copy(bf16[1,2,20480]{2,1,0:T(2,128)(2,1)} %param.6) | data formatting | bytes 163840 | tf_op args[1]
  1.8 12.0 %all_gather.3 = bf16[1,8,20480]{2,0,1:T(2,128)(2,1)S(1)} all-gather(bf16[1,2,20480]{2,0,1:T(2,128)(2,1)S(1)} %copy.17), channel_id=1, replica_groups=mesh['band'=4,'query'=8] {'band'}, dimensions={1}, use_global_device_ids=true | all-gather | bytes 409600 | tf_op jit(solution)/shard_map/all_gather | solution.py:50
  13.8 0.4 copy.28
  14.2 0.7 fusion.29
  14.9 34.0 %while.1 = (s32[]{:T(128)}, bf16[8,20736]{1,0:T(8,128)(2,1)S(1)}, s32[16,2]{0,1:T(2,128)S(1)}, bf16[16,8,20480]{2,1,0:T(8,128)(2,1)}, s32[]{:T(128)}) while((s32[]{:T(128)}, bf16[8,20736]{1,0:T(8,128)(2,1)S(1)}, s32[16,2]{0,1:T(2,128)S(1)}, bf16[16,8,20480]{2,1,0:T(8,128)(2,1)}, s32[]{:T(128)}) %tuple.24), condition=%wide.while_cond, body=%wide.while_body.sunk | while | flops 2 | bytes 655973 | solution.py:36
  15.0 0.5 slice.24
  15.5 1.5 %bitcast_dynamic-update-slice_fusion.2 = bf16[16,8,20480]{2,1,0:T(8,128)(2,1)} fusion(bf16[16,8,20480]{2,1,0:T(8,128)(2,1)} %get-tuple-element.58, s32[]{:T(128)S(6)} %copy.32, bf16[8,20736]{1,0:T(8,128)(2,1)S(1)} %get-tuple-element.61, s32[]{:T(128)} %bitcast.41), kind=kLoop, calls=%fused_computation.clone.1 | loop fusion | bytes 655876 | tf_op jit(solution)/shard_map/vmap()/gather
  17.1 0.5 slice.24
  17.6 1.5 %bitcast_dynamic-update-slice_fusion.2 = bf16[16,8,20480]{2,1,0:T(8,128)(2,1)} fusion(bf16[16,8,20480]{2,1,0:T(8,128)(2,1)} %get-tuple-element.58, s32[]{:T(128)S(6)} %copy.32, bf16[8,20736]{1,0:T(8,128)(2,1)S(1)} %get-tuple-element.61, s32[]{:T(128)} %bitcast.41), kind=kLoop, calls=%fused_computation.clone.1 | loop fusion | bytes 655876 | tf_op jit(solution)/shard_map/vmap()/gather
  19.2 0.5 slice.24
  19.8 1.5 %bitcast_dynamic-update-slice_fusion.2 = bf16[16,8,20480]{2,1,0:T(8,128)(2,1)} fusion(bf16[16,8,20480]{2,1,0:T(8,128)(2,1)} %get-tuple-element.58, s32[]{:T(128)S(6)} %copy.32, bf16[8,20736]{1,0:T(8,128)(2,1)S(1)} %get-tuple-element.61, s32[]{:T(128)} %bitcast.41), kind=kLoop, calls=%fused_computation.clone.1 | loop fusion | bytes 655876 | tf_op jit(solution)/shard_map/vmap()/gather
  21.4 0.5 slice.24
  21.9 1.5 %bitcast_dynamic-update-slice_fusion.2 = bf16[16,8,20480]{2,1,0:T(8,128)(2,1)} fusion(bf16[16,8,20480]{2,1,0:T(8,128)(2,1)} %get-tuple-element.58, s32[]{:T(128)S(6)} %copy.32, bf16[8,20736]{1,0:T(8,128)(2,1)S(1)} %get-tuple-element.61, s32[]{:T(128)} %bitcast.41), kind=kLoop, calls=%fused_computation.clone.1 | loop fusion | bytes 655876 | tf_op jit(solution)/shard_map/vmap()/gather
  23.5 0.5 slice.24
  24.0 1.5 %bitcast_dynamic-update-slice_fusion.2 = bf16[16,8,20480]{2,1,0:T(8,128)(2,1)} fusion(bf16[16,8,20480]{2,1,0:T(8,128)(2,1)} %get-tuple-element.58, s32[]{:T(128)S(6)} %copy.32, bf16[8,20736]{1,0:T(8,128)(2,1)S(1)} %get-tuple-element.61, s32[]{:T(128)} %bitcast.41), kind=kLoop, calls=%fused_computation.clone.1 | loop fusion | bytes 655876 | tf_op jit(solution)/shard_map/vmap()/gather
  25.6 0.5 slice.24
  26.1 1.5 %bitcast_dynamic-update-slice_fusion.2 = bf16[16,8,20480]{2,1,0:T(8,128)(2,1)} fusion(bf16[16,8,20480]{2,1,0:T(8,128)(2,1)} %get-tuple-element.58, s32[]{:T(128)S(6)} %copy.32, bf16[8,20736]{1,0:T(8,128)(2,1)S(1)} %get-tuple-element.61, s32[]{:T(128)} %bitcast.41), kind=kLoop, calls=%fused_computation.clone.1 | loop fusion | bytes 655876 | tf_op jit(solution)/shard_map/vmap()/gather
  27.7 0.5 slice.24
  28.2 1.6 %bitcast_dynamic-update-slice_fusion.2 = bf16[16,8,20480]{2,1,0:T(8,128)(2,1)} fusion(bf16[16,8,20480]{2,1,0:T(8,128)(2,1)} %get-tuple-element.58, s32[]{:T(128)S(6)} %copy.32, bf16[8,20736]{1,0:T(8,128)(2,1)S(1)} %get-tuple-element.61, s32[]{:T(128)} %bitcast.41), kind=kLoop, calls=%fused_computation.clone.1 | loop fusion | bytes 655876 | tf_op jit(solution)/shard_map/vmap()/gather
  29.9 0.5 slice.24
  30.4 1.5 %bitcast_dynamic-update-slice_fusion.2 = bf16[16,8,20480]{2,1,0:T(8,128)(2,1)} fusion(bf16[16,8,20480]{2,1,0:T(8,128)(2,1)} %get-tuple-element.58, s32[]{:T(128)S(6)} %copy.32, bf16[8,20736]{1,0:T(8,128)(2,1)S(1)} %get-tuple-element.61, s32[]{:T(128)} %bitcast.41), kind=kLoop, calls=%fused_computation.clone.1 | loop fusion | bytes 655876 | tf_op jit(solution)/shard_map/vmap()/gather
  32.0 0.5 slice.24
  32.5 1.5 %bitcast_dynamic-update-slice_fusion.2 = bf16[16,8,20480]{2,1,0:T(8,128)(2,1)} fusion(bf16[16,8,20480]{2,1,0:T(8,128)(2,1)} %get-tuple-element.58, s32[]{:T(128)S(6)} %copy.32, bf16[8,20736]{1,0:T(8,128)(2,1)S(1)} %get-tuple-element.61, s32[]{:T(128)} %bitcast.41), kind=kLoop, calls=%fused_computation.clone.1 | loop fusion | bytes 655876 | tf_op jit(solution)/shard_map/vmap()/gather
  34.1 0.5 slice.24
  34.6 1.5 %bitcast_dynamic-update-slice_fusion.2 = bf16[16,8,20480]{2,1,0:T(8,128)(2,1)} fusion(bf16[16,8,20480]{2,1,0:T(8,128)(2,1)} %get-tuple-element.58, s32[]{:T(128)S(6)} %copy.32, bf16[8,20736]{1,0:T(8,128)(2,1)S(1)} %get-tuple-element.61, s32[]{:T(128)} %bitcast.41), kind=kLoop, calls=%fused_computation.clone.1 | loop fusion | bytes 655876 | tf_op jit(solution)/shard_map/vmap()/gather
  36.2 0.5 slice.24
  36.8 1.5 %bitcast_dynamic-update-slice_fusion.2 = bf16[16,8,20480]{2,1,0:T(8,128)(2,1)} fusion(bf16[16,8,20480]{2,1,0:T(8,128)(2,1)} %get-tuple-element.58, s32[]{:T(128)S(6)} %copy.32, bf16[8,20736]{1,0:T(8,128)(2,1)S(1)} %get-tuple-element.61, s32[]{:T(128)} %bitcast.41), kind=kLoop, calls=%fused_computation.clone.1 | loop fusion | bytes 655876 | tf_op jit(solution)/shard_map/vmap()/gather
  38.4 0.5 slice.24
  38.9 1.5 %bitcast_dynamic-update-slice_fusion.2 = bf16[16,8,20480]{2,1,0:T(8,128)(2,1)} fusion(bf16[16,8,20480]{2,1,0:T(8,128)(2,1)} %get-tuple-element.58, s32[]{:T(128)S(6)} %copy.32, bf16[8,20736]{1,0:T(8,128)(2,1)S(1)} %get-tuple-element.61, s32[]{:T(128)} %bitcast.41), kind=kLoop, calls=%fused_computation.clone.1 | loop fusion | bytes 655876 | tf_op jit(solution)/shard_map/vmap()/gather
  40.5 0.5 slice.24
  41.0 1.5 %bitcast_dynamic-update-slice_fusion.2 = bf16[16,8,20480]{2,1,0:T(8,128)(2,1)} fusion(bf16[16,8,20480]{2,1,0:T(8,128)(2,1)} %get-tuple-element.58, s32[]{:T(128)S(6)} %copy.32, bf16[8,20736]{1,0:T(8,128)(2,1)S(1)} %get-tuple-element.61, s32[]{:T(128)} %bitcast.41), kind=kLoop, calls=%fused_computation.clone.1 | loop fusion | bytes 655876 | tf_op jit(solution)/shard_map/vmap()/gather
  42.6 0.5 slice.24
  43.1 1.5 %bitcast_dynamic-update-slice_fusion.2 = bf16[16,8,20480]{2,1,0:T(8,128)(2,1)} fusion(bf16[16,8,20480]{2,1,0:T(8,128)(2,1)} %get-tuple-element.58, s32[]{:T(128)S(6)} %copy.32, bf16[8,20736]{1,0:T(8,128)(2,1)S(1)} %get-tuple-element.61, s32[]{:T(128)} %bitcast.41), kind=kLoop, calls=%fused_computation.clone.1 | loop fusion | bytes 655876 | tf_op jit(solution)/shard_map/vmap()/gather
  44.7 0.5 slice.24
  45.2 1.5 %bitcast_dynamic-update-slice_fusion.2 = bf16[16,8,20480]{2,1,0:T(8,128)(2,1)} fusion(bf16[16,8,20480]{2,1,0:T(8,128)(2,1)} %get-tuple-element.58, s32[]{:T(128)S(6)} %copy.32, bf16[8,20736]{1,0:T(8,128)(2,1)S(1)} %get-tuple-element.61, s32[]{:T(128)} %bitcast.41), kind=kLoop, calls=%fused_computation.clone.1 | loop fusion | bytes 655876 | tf_op jit(solution)/shard_map/vmap()/gather
  46.8 0.5 slice.24
  47.3 1.5 %bitcast_dynamic-update-slice_fusion.2 = bf16[16,8,20480]{2,1,0:T(8,128)(2,1)} fusion(bf16[16,8,20480]{2,1,0:T(8,128)(2,1)} %get-tuple-element.58, s32[]{:T(128)S(6)} %copy.32, bf16[8,20736]{1,0:T(8,128)(2,1)S(1)} %get-tuple-element.61, s32[]{:T(128)} %bitcast.41), kind=kLoop, calls=%fused_computation.clone.1 | loop fusion | bytes 655876 | tf_op jit(solution)/shard_map/vmap()/gather
  49.2 1.2 %fusion.36 = (bf16[48,159,128]{2,1,0:T(8,128)(2,1)S(1)}, bf16[48,159,128]{2,1,0:T(8,128)(2,1)S(1)}) fusion(bf16[48,160,128]{2,1,0:T(8,128)(2,1)S(1)} %bitcast.42), kind=kLoop, calls=%fused_computation.47 | loop fusion | bytes 7815168 | tf_op jit(solution)/shard_map/slice | solution.py:23
  50.4 3.1 %subtract_convert_fusion = bf16[48,160,128]{2,1,0:T(8,128)(2,1)} fusion(bf16[48,160,128]{2,1,0:T(8,128)(2,1)S(1)} %bitcast.43, bf16[48,159,128]{2,1,0:T(8,128)(2,1)S(1)} %get-tuple-element.23, bf16[48,159,128]{2,1,0:T(8,128)(2,1)S(1)} %get-tuple-element.22, s32[384]{0:T(512)S(1)} %iota_add_fusion), kind=kOutput, calls=%fused_computation.16 | convolution fusion | flops 788643840 | bytes 7841280 | tf_op jit(solution)/shard_map/rbj,ji->rbi/dot_general | solution.py:26
  53.5 3.7 %dot_general.9 = bf16[8,6,20480]{2,1,0:T(8,128)(2,1)S(1)} reshape(bf16[48,160,128]{2,1,0:T(8,128)(2,1)} %subtract_convert_fusion) | data formatting | bytes 3932160 | tf_op jit(solution)/shard_map/mb,sb->ms/dot_general | solution.py:53
  57.3 13.3 %fusion.12 = f32[8,16,8,6]{2,0,3,1:T(8,128)S(1)} fusion(bf16[16,8,20480]{2,1,0:T(8,128)(2,1)} %get-tuple-element.9, bf16[8,6,20480]{2,1,0:T(8,128)(2,1)S(1)} %dot_general.9), kind=kOutput, calls=%fused_computation.14 | convolution fusion | flops 251658240 | bytes 7233536 | tf_op jit(solution)/shard_map/mb,sb->ms/dot_general | solution.py:53
  70.8 0.7 reshape.74
  71.6 4.9 %all-to-all-start = ((f32[8,1,768]{2,1,0:T(1,128)}), f32[8,1,768]{2,1,0:T(1,128)S(1)}, u32[]{:S(2)}, u32[]{:S(2)}) async-start(f32[8,1,768]{2,1,0:T(1,128)} %reshape.74), calls=%async_computation | async-start | bytes 49152 | tf_op jit(solution)/shard_map/all_to_all | solution.py:58
  76.6 5.5 %all-to-all-done = f32[8,1,768]{2,1,0:T(1,128)S(1)} async-done(((f32[8,1,768]{2,1,0:T(1,128)}), f32[8,1,768]{2,1,0:T(1,128)S(1)}, u32[]{:S(2)}, u32[]{:S(2)}) %all-to-all-start) | async-done | bytes 24608 | tf_op jit(solution)/shard_map/all_to_all | solution.py:58
  82.2 0.5 broadcast.91
  82.7 0.7 reduce.2
  83.5 0.7 fusion.20
  84.2 0.7 divide_bitcast_fusion
  (32 shorter events, 2.0 us)
Async XLA Ops:
  0.6 48.3 %copy-start = (bf16[48,20480]{1,0:T(8,128)(2,1)S(1)}, bf16[48,20480]{1,0:T(8,128)(2,1)}, u32[]{:S(2)}) copy-start(bf16[48,20480]{1,0:T(8,128)(2,1)} %param.5) | copy-start | bytes 5898244
  57.2 19.2 %copy-start.1 = (s32[48]{0:T(128)S(1)}, s32[48]{0:T(128)}, u32[]{:S(2)}) copy-start(s32[48]{0:T(128)} %param.9) | copy-start | bytes 580
  57.3 19.2 %copy-start.2 = (s32[48]{0:T(128)S(1)}, s32[48]{0:T(128)}, u32[]{:S(2)}) copy-start(s32[48]{0:T(128)} %param.8) | copy-start | bytes 580
  71.6 10.6 %all-to-all-start = ((f32[8,1,768]{2,1,0:T(1,128)}), f32[8,1,768]{2,1,0:T(1,128)S(1)}, u32[]{:S(2)}, u32[]{:S(2)}) async-start(f32[8,1,768]{2,1,0:T(1,128)} %reshape.74), calls=%async_computation | async-start | bytes 49152 | tf_op jit(solution)/shard_map/all_to_all | solution.py:58
where the time goes:
time: 85.3 us; the launch traced here: 84.9 us
  local copies, waits for them, and re-layouts  42.3 us (50%)
  matrix products  16.4 us (19%)
  blocking collectives  12 us (14%)
  waiting for transfers between devices  5.51 us (6%)
  starting transfers between devices  4.88 us (6%)
  other arithmetic  2.93 us (3%)
    gather x48, local copies, waits for them, and re-layouts  33.9 us
    dot_general x1, matrix products, local(): jnp.einsum('mb,sb->ms', copies, corrected, preferred_element_type=jnp.flo...  13.3 us
    all_gather x1, blocking collectives, local(): piece = lax.all_gather(theo, 'band', axis=1, tiled=True)  12 us
    all_to_all x1, waiting for transfers between devices, local(): lax.all_to_all(score_table, 'query', split_axis=2, concat_axis=0, tiled=T...  5.51 us
    all_to_all x1, starting transfers between devices, local(): lax.all_to_all(score_table, 'query', split_axis=2, concat_axis=0, tiled=T...  4.88 us
    dot_general x2, local copies, waits for them, and re-layouts, local(): jnp.einsum('mb,sb->ms', copies, corrected, preferred_element_type=jnp.flo...  3.95 us
    dot_general x1, matrix products, correct(): jnp.einsum('rbj,ji->rbi', stacked, box_table(), preferred_element_type=jn...  3.08 us
    unnamed x11, local copies, waits for them, and re-layouts  2.71 us
  transfers between devices with their start and end apart: 1, of which 1 were waited for; matrix products, arithmetic and copies ran while one was open for 0% of the time, Pallas kernels for 0%

commit v1 on v0

--- a/solution.py
+++ b/solution.py
@@ -55,7 +55,12 @@
     score_table = scores.reshape(group_size, shift_count, query_count, own_rows)
     low_own = lax.dynamic_slice_in_dim(win_lo, own_start, own_rows, 0)
     length_own = lax.dynamic_slice_in_dim(win_len, own_start, own_rows, 0)
-    gathered = lax.all_to_all(score_table, "query", split_axis=2, concat_axis=0, tiled=True)
+    gathered = jnp.concatenate(
+        lax.all_to_all(
+            jnp.stack(jnp.split(score_table, lax.axis_size("query"), axis=2)), "query", 0, 0
+        ),
+        axis=0,
+    )
     total_peptides = gathered.shape[0]
     owned_scores = gathered.reshape(total_peptides, shift_count, own_rows)
     peptide_index = lax.broadcasted_iota(jnp.int32, (total_peptides, own_rows), 0)

time: 85.3 us -> 89.4 us (1.048)
  matrix products: 16.4 us -> 19.9 us
  local copies, waits for them, and re-layouts: 42.3 us -> 43.5 us
    dot_general x1, matrix products: 13.3 us -> 16.8 us  [local(): jnp.einsum('mb,sb->ms', copies, corrected, preferred_element_type=jnp.flo...]
    unnamed x11 -> x20, local copies, waits for them, and re-layouts: 2.71 us -> 3.81 us
    dot_general x2 -> x1, local copies, waits for them, and re-layouts: 3.95 us -> 3.71 us  [local(): jnp.einsum('mb,sb->ms', copies, corrected, preferred_element_type=jnp.flo...]
where the time goes in v1:
time: 89.4 us; the launch traced here: 89 us
  local copies, waits for them, and re-layouts  43.5 us (49%)
  matrix products  19.9 us (22%)
  blocking collectives  12 us (13%)
  waiting for transfers between devices  5.51 us (6%)
  starting transfers between devices  4.87 us (5%)
  other arithmetic  2.27 us (3%)
    gather x48, local copies, waits for them, and re-layouts  33.9 us
    dot_general x1, matrix products, local(): jnp.einsum('mb,sb->ms', copies, corrected, preferred_element_type=jnp.flo...  16.8 us
    all_gather x1, blocking collectives, local(): piece = lax.all_gather(theo, 'band', axis=1, tiled=True)  12 us
    all_to_all x1, waiting for transfers between devices, local(): lax.all_to_all(jnp.stack(jnp.split(score_table, lax.axis_size('query'), a...  5.51 us
    all_to_all x1, starting transfers between devices, local(): lax.all_to_all(jnp.stack(jnp.split(score_table, lax.axis_size('query'), a...  4.87 us
    unnamed x20, local copies, waits for them, and re-layouts  3.81 us
    dot_general x1, local copies, waits for them, and re-layouts, local(): jnp.einsum('mb,sb->ms', copies, corrected, preferred_element_type=jnp.flo...  3.71 us
    dot_general x1, matrix products, correct(): jnp.einsum('rbj,ji->rbi', stacked, box_table(), preferred_element_type=jn...  3.08 us
  transfers between devices with their start and end apart: 1, of which 1 were waited for; matrix products, arithmetic and copies ran while one was open for 0% of the time, Pallas kernels for 0%

profile of v1, /device:TPU:0, one launch (start us, length us, event | category | flops | bytes accessed | tf_op | source)
XLA Modules:
  0.0 89.0 jit_solution(6712639845234634490)
XLA Ops:
  0.7 1.2 %copy.15 = bf16[1,2,20480]{2,0,1:T(2,128)(2,1)S(1)} copy(bf16[1,2,20480]{2,1,0:T(2,128)(2,1)} %param.6) | data formatting | bytes 163840 | tf_op args[1]
  1.8 12.0 %all_gather.3 = bf16[1,8,20480]{2,0,1:T(2,128)(2,1)S(1)} all-gather(bf16[1,2,20480]{2,0,1:T(2,128)(2,1)S(1)} %copy.15), channel_id=1, replica_groups=mesh['band'=4,'query'=8] {'band'}, dimensions={1}, use_global_device_ids=true | all-gather | bytes 409600 | tf_op jit(solution)/shard_map/all_gather | solution.py:50
  13.8 0.4 copy.33
  14.2 0.7 fusion.35
  14.9 34.0 %while.1 = (s32[]{:T(128)}, bf16[8,20736]{1,0:T(8,128)(2,1)S(1)}, s32[16,2]{0,1:T(2,128)S(1)}, bf16[16,8,20480]{2,1,0:T(8,128)(2,1)}, s32[]{:T(128)}) while((s32[]{:T(128)}, bf16[8,20736]{1,0:T(8,128)(2,1)S(1)}, s32[16,2]{0,1:T(2,128)S(1)}, bf16[16,8,20480]{2,1,0:T(8,128)(2,1)}, s32[]{:T(128)}) %tuple.25), condition=%wide.while_cond, body=%wide.while_body.sunk | while | flops 2 | bytes 655973 | solution.py:36
  15.0 0.5 slice.24
  15.5 1.5 %bitcast_dynamic-update-slice_fusion.2 = bf16[16,8,20480]{2,1,0:T(8,128)(2,1)} fusion(bf16[16,8,20480]{2,1,0:T(8,128)(2,1)} %get-tuple-element.60, s32[]{:T(128)S(6)} %copy.37, bf16[8,20736]{1,0:T(8,128)(2,1)S(1)} %get-tuple-element.63, s32[]{:T(128)} %bitcast.65), kind=kLoop, calls=%fused_computation.clone.1 | loop fusion | bytes 655876 | tf_op jit(solution)/shard_map/vmap()/gather
  17.1 0.5 slice.24
  17.6 1.5 %bitcast_dynamic-update-slice_fusion.2 = bf16[16,8,20480]{2,1,0:T(8,128)(2,1)} fusion(bf16[16,8,20480]{2,1,0:T(8,128)(2,1)} %get-tuple-element.60, s32[]{:T(128)S(6)} %copy.37, bf16[8,20736]{1,0:T(8,128)(2,1)S(1)} %get-tuple-element.63, s32[]{:T(128)} %bitcast.65), kind=kLoop, calls=%fused_computation.clone.1 | loop fusion | bytes 655876 | tf_op jit(solution)/shard_map/vmap()/gather
  19.2 0.5 slice.24
  19.8 1.5 %bitcast_dynamic-update-slice_fusion.2 = bf16[16,8,20480]{2,1,0:T(8,128)(2,1)} fusion(bf16[16,8,20480]{2,1,0:T(8,128)(2,1)} %get-tuple-element.60, s32[]{:T(128)S(6)} %copy.37, bf16[8,20736]{1,0:T(8,128)(2,1)S(1)} %get-tuple-element.63, s32[]{:T(128)} %bitcast.65), kind=kLoop, calls=%fused_computation.clone.1 | loop fusion | bytes 655876 | tf_op jit(solution)/shard_map/vmap()/gather
  21.4 0.5 slice.24
  21.9 1.5 %bitcast_dynamic-update-slice_fusion.2 = bf16[16,8,20480]{2,1,0:T(8,128)(2,1)} fusion(bf16[16,8,20480]{2,1,0:T(8,128)(2,1)} %get-tuple-element.60, s32[]{:T(128)S(6)} %copy.37, bf16[8,20736]{1,0:T(8,128)(2,1)S(1)} %get-tuple-element.63, s32[]{:T(128)} %bitcast.65), kind=kLoop, calls=%fused_computation.clone.1 | loop fusion | bytes 655876 | tf_op jit(solution)/shard_map/vmap()/gather
  23.5 0.5 slice.24
  24.0 1.5 %bitcast_dynamic-update-slice_fusion.2 = bf16[16,8,20480]{2,1,0:T(8,128)(2,1)} fusion(bf16[16,8,20480]{2,1,0:T(8,128)(2,1)} %get-tuple-element.60, s32[]{:T(128)S(6)} %copy.37, bf16[8,20736]{1,0:T(8,128)(2,1)S(1)} %get-tuple-element.63, s32[]{:T(128)} %bitcast.65), kind=kLoop, calls=%fused_computation.clone.1 | loop fusion | bytes 655876 | tf_op jit(solution)/shard_map/vmap()/gather
  25.6 0.5 slice.24
  26.1 1.5 %bitcast_dynamic-update-slice_fusion.2 = bf16[16,8,20480]{2,1,0:T(8,128)(2,1)} fusion(bf16[16,8,20480]{2,1,0:T(8,128)(2,1)} %get-tuple-element.60, s32[]{:T(128)S(6)} %copy.37, bf16[8,20736]{1,0:T(8,128)(2,1)S(1)} %get-tuple-element.63, s32[]{:T(128)} %bitcast.65), kind=kLoop, calls=%fused_computation.clone.1 | loop fusion | bytes 655876 | tf_op jit(solution)/shard_map/vmap()/gather
  27.7 0.5 slice.24
  28.2 1.6 %bitcast_dynamic-update-slice_fusion.2 = bf16[16,8,20480]{2,1,0:T(8,128)(2,1)} fusion(bf16[16,8,20480]{2,1,0:T(8,128)(2,1)} %get-tuple-element.60, s32[]{:T(128)S(6)} %copy.37, bf16[8,20736]{1,0:T(8,128)(2,1)S(1)} %get-tuple-element.63, s32[]{:T(128)} %bitcast.65), kind=kLoop, calls=%fused_computation.clone.1 | loop fusion | bytes 655876 | tf_op jit(solution)/shard_map/vmap()/gather
  29.9 0.5 slice.24
  30.4 1.5 %bitcast_dynamic-update-slice_fusion.2 = bf16[16,8,20480]{2,1,0:T(8,128)(2,1)} fusion(bf16[16,8,20480]{2,1,0:T(8,128)(2,1)} %get-tuple-element.60, s32[]{:T(128)S(6)} %copy.37, bf16[8,20736]{1,0:T(8,128)(2,1)S(1)} %get-tuple-element.63, s32[]{:T(128)} %bitcast.65), kind=kLoop, calls=%fused_computation.clone.1 | loop fusion | bytes 655876 | tf_op jit(solution)/shard_map/vmap()/gather
  32.0 0.5 slice.24
  32.5 1.5 %bitcast_dynamic-update-slice_fusion.2 = bf16[16,8,20480]{2,1,0:T(8,128)(2,1)} fusion(bf16[16,8,20480]{2,1,0:T(8,128)(2,1)} %get-tuple-element.60, s32[]{:T(128)S(6)} %copy.37, bf16[8,20736]{1,0:T(8,128)(2,1)S(1)} %get-tuple-element.63, s32[]{:T(128)} %bitcast.65), kind=kLoop, calls=%fused_computation.clone.1 | loop fusion | bytes 655876 | tf_op jit(solution)/shard_map/vmap()/gather
  34.1 0.5 slice.24
  34.6 1.5 %bitcast_dynamic-update-slice_fusion.2 = bf16[16,8,20480]{2,1,0:T(8,128)(2,1)} fusion(bf16[16,8,20480]{2,1,0:T(8,128)(2,1)} %get-tuple-element.60, s32[]{:T(128)S(6)} %copy.37, bf16[8,20736]{1,0:T(8,128)(2,1)S(1)} %get-tuple-element.63, s32[]{:T(128)} %bitcast.65), kind=kLoop, calls=%fused_computation.clone.1 | loop fusion | bytes 655876 | tf_op jit(solution)/shard_map/vmap()/gather
  36.2 0.5 slice.24
  36.8 1.5 %bitcast_dynamic-update-slice_fusion.2 = bf16[16,8,20480]{2,1,0:T(8,128)(2,1)} fusion(bf16[16,8,20480]{2,1,0:T(8,128)(2,1)} %get-tuple-element.60, s32[]{:T(128)S(6)} %copy.37, bf16[8,20736]{1,0:T(8,128)(2,1)S(1)} %get-tuple-element.63, s32[]{:T(128)} %bitcast.65), kind=kLoop, calls=%fused_computation.clone.1 | loop fusion | bytes 655876 | tf_op jit(solution)/shard_map/vmap()/gather
  38.4 0.5 slice.24
  38.9 1.5 %bitcast_dynamic-update-slice_fusion.2 = bf16[16,8,20480]{2,1,0:T(8,128)(2,1)} fusion(bf16[16,8,20480]{2,1,0:T(8,128)(2,1)} %get-tuple-element.60, s32[]{:T(128)S(6)} %copy.37, bf16[8,20736]{1,0:T(8,128)(2,1)S(1)} %get-tuple-element.63, s32[]{:T(128)} %bitcast.65), kind=kLoop, calls=%fused_computation.clone.1 | loop fusion | bytes 655876 | tf_op jit(solution)/shard_map/vmap()/gather
  40.5 0.5 slice.24
  41.0 1.5 %bitcast_dynamic-update-slice_fusion.2 = bf16[16,8,20480]{2,1,0:T(8,128)(2,1)} fusion(bf16[16,8,20480]{2,1,0:T(8,128)(2,1)} %get-tuple-element.60, s32[]{:T(128)S(6)} %copy.37, bf16[8,20736]{1,0:T(8,128)(2,1)S(1)} %get-tuple-element.63, s32[]{:T(128)} %bitcast.65), kind=kLoop, calls=%fused_computation.clone.1 | loop fusion | bytes 655876 | tf_op jit(solution)/shard_map/vmap()/gather
  42.6 0.5 slice.24
  43.1 1.5 %bitcast_dynamic-update-slice_fusion.2 = bf16[16,8,20480]{2,1,0:T(8,128)(2,1)} fusion(bf16[16,8,20480]{2,1,0:T(8,128)(2,1)} %get-tuple-element.60, s32[]{:T(128)S(6)} %copy.37, bf16[8,20736]{1,0:T(8,128)(2,1)S(1)} %get-tuple-element.63, s32[]{:T(128)} %bitcast.65), kind=kLoop, calls=%fused_computation.clone.1 | loop fusion | bytes 655876 | tf_op jit(solution)/shard_map/vmap()/gather
  44.7 0.5 slice.24
  45.2 1.5 %bitcast_dynamic-update-slice_fusion.2 = bf16[16,8,20480]{2,1,0:T(8,128)(2,1)} fusion(bf16[16,8,20480]{2,1,0:T(8,128)(2,1)} %get-tuple-element.60, s32[]{:T(128)S(6)} %copy.37, bf16[8,20736]{1,0:T(8,128)(2,1)S(1)} %get-tuple-element.63, s32[]{:T(128)} %bitcast.65), kind=kLoop, calls=%fused_computation.clone.1 | loop fusion | bytes 655876 | tf_op jit(solution)/shard_map/vmap()/gather
  46.8 0.5 slice.24
  47.3 1.5 %bitcast_dynamic-update-slice_fusion.2 = bf16[16,8,20480]{2,1,0:T(8,128)(2,1)} fusion(bf16[16,8,20480]{2,1,0:T(8,128)(2,1)} %get-tuple-element.60, s32[]{:T(128)S(6)} %copy.37, bf16[8,20736]{1,0:T(8,128)(2,1)S(1)} %get-tuple-element.63, s32[]{:T(128)} %bitcast.65), kind=kLoop, calls=%fused_computation.clone.1 | loop fusion | bytes 655876 | tf_op jit(solution)/shard_map/vmap()/gather
  49.2 1.2 %fusion.42 = (bf16[48,159,128]{2,1,0:T(8,128)(2,1)S(1)}, bf16[48,159,128]{2,1,0:T(8,128)(2,1)S(1)}) fusion(bf16[48,160,128]{2,1,0:T(8,128)(2,1)S(1)} %bitcast.66), kind=kLoop, calls=%fused_computation.61 | loop fusion | bytes 7815168 | tf_op jit(solution)/shard_map/slice | solution.py:23
  50.4 3.1 %subtract_convert_fusion = bf16[48,160,128]{2,1,0:T(8,128)(2,1)} fusion(bf16[48,160,128]{2,1,0:T(8,128)(2,1)S(1)} %bitcast.67, bf16[48,159,128]{2,1,0:T(8,128)(2,1)S(1)} %get-tuple-element.25, bf16[48,159,128]{2,1,0:T(8,128)(2,1)S(1)} %get-tuple-element.24, s32[384]{0:T(512)S(1)} %iota_add_fusion), kind=kOutput, calls=%fused_computation.16 | convolution fusion | flops 788643840 | bytes 7841280 | tf_op jit(solution)/shard_map/rbj,ji->rbi/dot_general | solution.py:26
  53.5 3.7 %dot_general.9 = bf16[8,6,20480]{2,1,0:T(8,128)(2,1)S(1)} reshape(bf16[48,160,128]{2,1,0:T(8,128)(2,1)} %subtract_convert_fusion) | data formatting | bytes 3932160 | tf_op jit(solution)/shard_map/mb,sb->ms/dot_general | solution.py:53
  57.3 16.8 %fusion.12 = f32[8,16,8,6]{0,2,3,1:T(8,128)S(1)} fusion(bf16[16,8,20480]{2,1,0:T(8,128)(2,1)} %get-tuple-element.9, bf16[8,6,20480]{2,1,0:T(8,128)(2,1)S(1)} %dot_general.9), kind=kOutput, calls=%fused_computation.14 | convolution fusion | flops 251658240 | bytes 7233536 | tf_op jit(solution)/shard_map/mb,sb->ms/dot_general | solution.py:53
  74.8 0.7 reshape.72
  75.5 4.9 %all-to-all-start = ((f32[8,1,768]{2,1,0:T(1,128)}), f32[8,1,768]{2,1,0:T(1,128)S(1)}, u32[]{:S(2)}, u32[]{:S(2)}) async-start(f32[8,1,768]{2,1,0:T(1,128)} %reshape.72), calls=%async_computation | async-start | bytes 49152 | tf_op jit(solution)/shard_map/all_to_all | solution.py:59
  80.6 5.5 %all-to-all-done = f32[8,1,768]{2,1,0:T(1,128)S(1)} async-done(((f32[8,1,768]{2,1,0:T(1,128)}), f32[8,1,768]{2,1,0:T(1,128)S(1)}, u32[]{:S(2)}, u32[]{:S(2)}) %all-to-all-start) | async-done | bytes 24608 | tf_op jit(solution)/shard_map/all_to_all | solution.py:59
  86.1 0.5 broadcast.91
  86.6 0.7 reduce.2
  87.5 0.7 select_reduce_fusion
  88.3 0.7 copy.21
  (42 shorter events, 2.6 us)
Async XLA Ops:
  0.6 48.3 %copy-start = (bf16[48,20480]{1,0:T(8,128)(2,1)S(1)}, bf16[48,20480]{1,0:T(8,128)(2,1)}, u32[]{:S(2)}) copy-start(bf16[48,20480]{1,0:T(8,128)(2,1)} %param.5) | copy-start | bytes 5898244
  57.2 23.2 %copy-start.1 = (s32[48]{0:T(128)S(1)}, s32[48]{0:T(128)}, u32[]{:S(2)}) copy-start(s32[48]{0:T(128)} %param.9) | copy-start | bytes 580
  57.3 23.2 %copy-start.2 = (s32[48]{0:T(128)S(1)}, s32[48]{0:T(128)}, u32[]{:S(2)}) copy-start(s32[48]{0:T(128)} %param.8) | copy-start | bytes 580
  75.5 10.6 %all-to-all-start = ((f32[8,1,768]{2,1,0:T(1,128)}), f32[8,1,768]{2,1,0:T(1,128)S(1)}, u32[]{:S(2)}, u32[]{:S(2)}) async-start(f32[8,1,768]{2,1,0:T(1,128)} %reshape.72), calls=%async_computation | async-start | bytes 49152 | tf_op jit(solution)/shard_map/all_to_all | solution.py:59
